TPU v7x, 256 devices: a whole 4x4x8 slice. The times are simulated.
256 devices in a mesh: energy: 32 (over x, y, core), cell: 8 (over z).
Axes of the slice: x: 4, y: 4, z: 8, core: 2. Of those that a mesh axis runs over, the one named last changes fastest.
Arguments:
- retarded_diag: bfloat16 [2, 64, 32, 256, 256], P(None, 'energy', 'cell'), may hold values from -0.375 to 0.375
- retarded_lower: bfloat16 [2, 64, 32, 256, 256], P(None, 'energy', 'cell'), may hold values from -0.375 to 0.375
- retarded_upper: bfloat16 [2, 64, 32, 256, 256], P(None, 'energy', 'cell'), may hold values from -0.375 to 0.375
- sigma_lesser: bfloat16 [2, 64, 32, 256, 256], P(None, 'energy', 'cell'), may hold values from -6 to 6
- screened: bfloat16 [2, 32, 128], P(None, 'cell'), may hold values from -0.5 to 0.5
- kept: int32 [32, 8], P('cell'), may hold values from 0 to 15, as said below
- kept_count: int32 [32], P('cell'), may hold values from 1 to 8, as said below
Outputs:
- sigma_new: bfloat16 [2, 64, 32, 8, 4096], P(None, 'energy', 'cell')
Inputs may be any that keep to these rules, and one draw needn't show every extreme that they name: `kept`: each row holds 8 different sub-block numbers. `kept_count`: some cell has 8 live slots and some other cell 1.
All inputs are finite; a program needn't handle non-finite values.
Results may differ from a plain program's by a relative error of at most 0.0057.
Values may be sent and summed in bfloat16 or wider, within the bound.
A program may use at most 128 MiB of HBM per device.

v0:
```python
from functools import partial

import jax
import jax.numpy as jnp
from jax import lax
from jax.sharding import PartitionSpec as P

ORB = 256
SUB = 64
KMAX = 8


def with_halo(block, sides, width):
    for axis, dim in sides:
        count = lax.axis_size(axis)
        forward = [(i, i + 1) for i in range(count - 1)]
        backward = [(target, source) for source, target in forward]
        low = lax.ppermute(
            lax.slice_in_dim(block, block.shape[dim] - width, None, axis=dim), axis, forward
        )
        high = lax.ppermute(lax.slice_in_dim(block, 0, width, axis=dim), axis, backward)
        block = jnp.concatenate([low, block, high], axis=dim)
    return block


def batched(left_side, right_side):
    return jnp.einsum("ecij,ecjk->ecik", left_side, right_side, preferred_element_type=jnp.float32)


def strips(hot, blocks):
    shaped = blocks.reshape(blocks.shape[0], blocks.shape[1], hot.shape[2], SUB, blocks.shape[3])
    return jnp.einsum("ckp,ecpij->eckij", hot, shaped, preferred_element_type=jnp.float32).astype(
        jnp.bfloat16
    )


def outer_part(left_side, right_side):
    return jnp.einsum(
        "eckij,eckqj->cekiq", left_side, right_side, preferred_element_type=jnp.float32
    )


def kept_sandwich(row_hot, col_hot, factor, middle):
    inner_r = (batched(factor[0], middle[0]) - batched(factor[1], middle[1])).astype(jnp.bfloat16)
    inner_i = (batched(factor[0], middle[1]) + batched(factor[1], middle[0])).astype(jnp.bfloat16)
    rows_r = strips(row_hot, inner_r)
    rows_i = strips(row_hot, inner_i)
    factor_r = strips(col_hot, factor[0])
    factor_i = strips(col_hot, factor[1])
    outer_r = outer_part(rows_r, factor_r) + outer_part(rows_i, factor_i)
    outer_i = outer_part(rows_i, factor_r) - outer_part(rows_r, factor_i)
    return (outer_r, outer_i)


def toeplitz(screened):
    energy_count = screened.shape[2] // 2
    position = jnp.arange(energy_count, dtype=jnp.int32)
    offsets = position[:, None] - position[None, :] + energy_count - 1
    return jnp.take(screened, offsets, axis=2)


def convolve(kernel, chosen):
    shape_in = chosen.shape
    flat = chosen.reshape(2, shape_in[1], shape_in[2], shape_in[3] * shape_in[4])
    form = "cef,cfm->cem"
    real_part = jnp.einsum(
        form, kernel[0], flat[0], preferred_element_type=jnp.float32
    ) - jnp.einsum(form, kernel[1], flat[1], preferred_element_type=jnp.float32)
    imag_part = jnp.einsum(
        form, kernel[0], flat[1], preferred_element_type=jnp.float32
    ) + jnp.einsum(form, kernel[1], flat[0], preferred_element_type=jnp.float32)
    return jnp.stack([real_part, imag_part]).astype(jnp.bfloat16).reshape(shape_in)


def per_device(
    retarded_diag, retarded_lower, retarded_upper, sigma_lesser, screened, kept, kept_count
):
    padded = with_halo(sigma_lesser, (("cell", 2),), 1)
    cell_count = sigma_lesser.shape[2]
    prev_cell = padded[:, :, 0:cell_count]
    next_cell = padded[:, :, 2 : cell_count + 2]
    per_side = ORB // SUB
    sides = jnp.arange(per_side, dtype=jnp.int32)
    row_hot = ((kept // per_side)[:, :, None] == sides[None, None, :]).astype(jnp.bfloat16)
    col_hot = ((kept % per_side)[:, :, None] == sides[None, None, :]).astype(jnp.bfloat16)
    first_r, first_i = kept_sandwich(row_hot, col_hot, retarded_diag, sigma_lesser)
    second_r, second_i = kept_sandwich(row_hot, col_hot, retarded_lower, prev_cell)
    third_r, third_i = kept_sandwich(row_hot, col_hot, retarded_upper, next_cell)
    lesser = jnp.stack([first_r + second_r + third_r, first_i + second_i + third_i]).astype(
        jnp.bfloat16
    )
    lesser = lesser.reshape(lesser.shape[:4] + (SUB * SUB,))
    live_slots = (jnp.arange(KMAX, dtype=jnp.int32)[None, :] < kept_count[:, None]).astype(
        jnp.bfloat16
    )
    chosen = lesser * live_slots[None, :, None, :, None]
    kernel = toeplitz(screened)
    mapper = partial(convolve, kernel)
    convolved = mapper(lax.all_to_all(chosen, "energy", split_axis=4, concat_axis=2, tiled=True))
    result = lax.all_to_all(convolved, "energy", split_axis=2, concat_axis=4, tiled=True)
    return jnp.swapaxes(result, 1, 2)


def solution(mesh):
    placed = (
        P(None, "energy", "cell", None, None),
        P(None, "energy", "cell", None, None),
        P(None, "energy", "cell", None, None),
        P(None, "energy", "cell", None, None),
        P(None, "cell", None),
        P("cell", None),
        P("cell"),
    )
    return jax.shard_map(
        per_device,
        mesh=mesh,
        in_specs=placed,
        out_specs=P(None, "energy", "cell", None, None),
        check_vma=False,
    )
```

profile of v0, /device:TPU:1, one launch (start us, length us, event | category | flops | bytes accessed | tf_op | source)
XLA Modules:
  0.0 208.7 jit_solution(11229530620356024958)
XLA Ops:
  0.0 1.4 fusion.119
  1.4 4.4 %collective-permute-start = (bf16[2,2,1,256,256]{4,3,2,1,0:T(8,128)(2,1)S(1)}, bf16[2,2,1,256,256]{4,3,2,1,0:T(8,128)(2,1)S(1)}, u32[]{:S(2)}, u32[]{:S(2)}) collective-permute-start(bf16[2,2,1,256,256]{4,3,2,1,0:T(8,128)(2,1)S(1)} %get-tuple-element.11), channel_id=1, source_target_pairs={{0,1},{1,2},{2,3},{3,4},{4,5},{5,6},{6,7},{8,9},{9,10},{10,11},{11... | collective-permute-start | bytes 1572872 | tf_op jit(solution)/shard_map/ppermute | solution.py:18
  5.8 1.4 collective-permute-start.1
  7.3 1.7 fusion.58
  11.9 0.9 convert_bitcast_fusion.11
  12.9 1.1 convert_bitcast_fusion.8
  14.0 1.1 convert_bitcast_fusion.10
  15.1 2.2 %fusion.24 = f32[4,2,8,64,64]{4,3,2,1,0:T(8,128)} fusion(bf16[2,4,8,64,256]{4,2,3,0,1:T(8,128)(2,1)S(1)} %convert_bitcast_fusion.8, bf16[2,4,8,64,256]{4,2,3,0,1:T(8,128)(2,1)S(1)} %convert_bitcast_fusion.11), kind=kOutput, calls=%fused_computation.45 | convolution fusion | flops 134217728 | bytes 5242880 | tf_op jit(solution)/shard_map/eckij,eckqj->cekiq/dot_general | solution.py:38
  19.1 1.1 convert_bitcast_fusion.6
  20.2 1.1 convert_bitcast_fusion.4
  22.0 1.1 convert_bitcast_fusion.2
  23.1 1.3 convert_bitcast_fusion
  26.4 0.9 convert_bitcast_fusion.3
  27.3 2.1 %fusion = f32[4,2,8,64,64]{4,3,2,1,0:T(8,128)} fusion(bf16[2,4,8,64,256]{4,2,3,0,1:T(8,128)(2,1)S(1)} %convert_bitcast_fusion, bf16[2,4,8,64,256]{4,2,3,0,1:T(8,128)(2,1)S(1)} %convert_bitcast_fusion.3), kind=kOutput, calls=%fused_computation.21 | convolution fusion | flops 134217728 | bytes 5242880 | tf_op jit(solution)/shard_map/eckij,eckqj->cekiq/dot_general | solution.py:38
  31.7 2.1 %fusion.4 = f32[4,2,8,64,64]{4,3,2,1,0:T(8,128)} fusion(bf16[2,4,8,64,256]{4,2,3,0,1:T(8,128)(2,1)S(1)} %convert_bitcast_fusion.1, bf16[2,4,8,64,256]{4,2,3,0,1:T(8,128)(2,1)S(1)} %convert_bitcast_fusion.2), kind=kOutput, calls=%fused_computation.25 | convolution fusion | flops 134217728 | bytes 5242880 | tf_op jit(solution)/shard_map/eckij,eckqj->cekiq/dot_general | solution.py:38
  35.9 0.9 convert_bitcast_fusion.7
  36.9 2.2 %fusion.12 = f32[4,2,8,64,64]{4,3,2,1,0:T(8,128)} fusion(bf16[2,4,8,64,256]{4,2,3,0,1:T(8,128)(2,1)S(1)} %convert_bitcast_fusion.4, bf16[2,4,8,64,256]{4,2,3,0,1:T(8,128)(2,1)S(1)} %convert_bitcast_fusion.7), kind=kOutput, calls=%fused_computation.33 | convolution fusion | flops 134217728 | bytes 5242880 | tf_op jit(solution)/shard_map/eckij,eckqj->cekiq/dot_general | solution.py:38
  41.2 2.4 %fusion.16 = f32[4,2,8,64,64]{4,3,2,1,0:T(8,128)} fusion(bf16[2,4,8,64,256]{4,2,3,0,1:T(8,128)(2,1)S(1)} %convert_bitcast_fusion.5, bf16[2,4,8,64,256]{4,2,3,0,1:T(8,128)(2,1)S(1)} %convert_bitcast_fusion.6), kind=kOutput, calls=%fused_computation.37 | convolution fusion | flops 134217728 | bytes 5242880 | tf_op jit(solution)/shard_map/eckij,eckqj->cekiq/dot_general | solution.py:38
  44.4 1.3 add_convert_fusion.1
  45.7 1.6 stack.18
  47.4 6.0 %add_convert_fusion = bf16[4,2,8,64,64]{4,3,2,1,0:T(8,128)(2,1)S(1)} fusion(f32[4,2,8,64,64]{4,3,2,1,0:T(8,128)} %fusion.4, f32[4,2,8,64,64]{4,3,2,1,0:T(8,128)} %fusion, f32[4,2,8,64,64]{4,3,2,1,0:T(8,128)} %fusion.16, f32[4,2,8,64,64]{4,3,2,1,0:T(8,128)} %fusion.12, f32[4,2,8,64,64]{4,3,2,1,0:T(8,128)} %fusion.24, ...), kind=kOutput, calls=%fused_computation.1 | convolution fusion | flops 135790592 | bytes 9961472 | tf_op jit(solution)/shard_map/eckij,eckqj->cekiq/dot_general | solution.py:38
  54.2 1.2 maximum_multiply_fusion
  55.4 28.1 %copy.169 = bf16[2,4,2,8,4096]{3,2,1,0,4:T(2,128)(2,1)} copy(bf16[2,4,2,8,4096]{4,3,2,1,0:T(8,128)(2,1)S(1)} %maximum_multiply_fusion) | data formatting | bytes 2097152 | tf_op jit(solution)/shard_map/mul | solution.py:96
  83.4 20.6 %reshape.121 = bf16[32,2,8192]{2,1,0:T(2,128)(2,1)} reshape(bf16[4096,2,4,2,8]{4,3,2,1,0:T(2,128)(2,1)} %bitcast.165) | data formatting | bytes 2097152
  104.0 8.2 %all-to-all-start = ((bf16[32,2,8192]{2,1,0:T(2,128)(2,1)}), bf16[32,2,8192]{2,1,0:T(2,128)(2,1)S(1)}, u32[]{:S(2)}, u32[]{:S(2)}) async-start(bf16[32,2,8192]{2,1,0:T(2,128)(2,1)} %reshape.121), calls=%async_computation | async-start | bytes 2097152 | tf_op jit(solution)/shard_map/all_to_all | solution.py:99
  112.5 13.8 %gather_fusion = bf16[4096,2,4]{2,1,0:T(2,128)(2,1)S(1)} fusion(bf16[2,4,128]{1,0,2:T(2,128)(2,1)S(1)} %copy.130, s32[4096]{0:T(1024)S(1)} %broadcast_clamp_fusion), kind=kCustom, calls=%fused_computation | custom fusion | bytes 147456 | tf_op jit(solution)/shard_map/jit(_take)/gather | solution.py:59
  126.2 1.8 copy.176
  128.1 1.0 all-to-all-done
  129.1 20.8 %reshape.122 = bf16[4096,2,4,2,8]{4,3,2,1,0:T(2,128)(2,1)} reshape(bf16[32,2,8192]{2,1,0:T(2,128)(2,1)S(1)} %all-to-all-done) | data formatting | bytes 2097152
  149.9 32.1 %copy.170 = bf16[2,4,2,8,32,128]{5,3,2,4,1,0:T(8,128)(2,1)S(1)} copy(bf16[2,4,2,8,32,128]{3,2,1,0,5,4:T(2,128)(2,1)} %bitcast.166) | data formatting | bytes 2097152 | tf_op jit(solution)/shard_map/all_to_all | solution.py:99
  184.4 23.1 %all_to_all.33 = bf16[2,4,64,8,128]{4,3,1,0,2:T(8,128)(2,1)S(1)} all-to-all(bf16[2,4,64,8,128]{4,3,1,0,2:T(8,128)(2,1)S(1)} %copy.177), channel_id=1, replica_groups=mesh['energy'=32,'cell'=8] {'energy'}, dimensions={2} | all-to-all | bytes 2097152 | tf_op jit(solution)/shard_map/all_to_all | solution.py:100
  207.5 1.2 copy.262
  (63 shorter events, 17.9 us)
Async XLA Ops:
  0.0 7.3 %copy-start = (bf16[2,2,4,256,256]{4,3,2,1,0:T(8,128)(2,1)S(1)}, bf16[2,2,4,256,256]{4,3,2,1,0:T(8,128)(2,1)}, u32[]{:S(2)}) copy-start(bf16[2,2,4,256,256]{4,3,2,1,0:T(8,128)(2,1)} %param.10) | copy-start | bytes 6291460
  1.4 23.1 %collective-permute-start = (bf16[2,2,1,256,256]{4,3,2,1,0:T(8,128)(2,1)S(1)}, bf16[2,2,1,256,256]{4,3,2,1,0:T(8,128)(2,1)S(1)}, u32[]{:S(2)}, u32[]{:S(2)}) collective-permute-start(bf16[2,2,1,256,256]{4,3,2,1,0:T(8,128)(2,1)S(1)} %get-tuple-element.11), channel_id=1, source_target_pairs={{0,1},{1,2},{2,3},{3,4},{4,5},{5,6},{6,7},{8,9},{9,10},{10,11},{11... | collective-permute-start | bytes 1572872 | tf_op jit(solution)/shard_map/ppermute | solution.py:18
  5.8 3.1 %copy-start.1 = (bf16[2,2,4,256,256]{4,3,2,1,0:T(8,128)(2,1)S(1)}, bf16[2,2,4,256,256]{4,3,2,1,0:T(8,128)(2,1)}, u32[]{:S(2)}) copy-start(bf16[2,2,4,256,256]{4,3,2,1,0:T(8,128)(2,1)} %param.7) | copy-start | bytes 6291460
  5.8 19.2 %collective-permute-start.1 = (bf16[2,2,1,256,256]{4,3,2,1,0:T(8,128)(2,1)S(1)}, bf16[2,2,1,256,256]{4,3,2,1,0:T(8,128)(2,1)S(1)}, u32[]{:S(2)}, u32[]{:S(2)}) collective-permute-start(bf16[2,2,1,256,256]{4,3,2,1,0:T(8,128)(2,1)S(1)} %get-tuple-element.12), channel_id=1, source_target_pairs={{1,0},{2,1},{3,2},{4,3},{5,4},{6,5},{7,6},{9,8},{10,9},{11,10},{12... | collective-permute-start | bytes 1572872 | tf_op jit(solution)/shard_map/ppermute | solution.py:21
  9.4 0.7 copy-start.5
  11.9 5.4 %copy-start.4 = (bf16[2,4,8,64,256]{4,2,3,0,1:T(8,128)(2,1)}, bf16[2,4,8,64,256]{4,2,3,0,1:T(8,128)(2,1)S(1)}, u32[]{:S(2)}) copy-start(bf16[2,4,8,64,256]{4,2,3,0,1:T(8,128)(2,1)S(1)} %convert_bitcast_fusion.9) | copy-start | bytes 6291460
  17.3 1.6 copy-start.3
  20.2 1.6 copy-start.2
  23.1 1.3 copy-start.7
  104.0 8.3 %copy-start.6 = (bf16[2,4,128]{2,1,0:T(4,128)(2,1)S(1)}, bf16[2,4,128]{2,1,0:T(4,128)(2,1)}, u32[]{:S(2)}) copy-start(bf16[2,4,128]{2,1,0:T(4,128)(2,1)} %param.11) | copy-start | bytes 6148
  104.0 25.1 %all-to-all-start = ((bf16[32,2,8192]{2,1,0:T(2,128)(2,1)}), bf16[32,2,8192]{2,1,0:T(2,128)(2,1)S(1)}, u32[]{:S(2)}, u32[]{:S(2)}) async-start(bf16[32,2,8192]{2,1,0:T(2,128)(2,1)} %reshape.121), calls=%async_computation | async-start | bytes 2097152 | tf_op jit(solution)/shard_map/all_to_all | solution.py:99
where the time goes:
time: 211 us; the launch traced here: 209 us
  local copies, waits for them, and re-layouts  126 us (60%)
  matrix products  42.3 us (20%)
  blocking collectives  23.1 us (11%)
  starting transfers between devices  14 us (7%)
    unnamed x22, local copies, waits for them, and re-layouts  43.6 us
    all_to_all x1, local copies, waits for them, and re-layouts, per_device(): lax.all_to_all(chosen, 'energy', split_axis=4, concat_axis=2, tiled=True)  32.1 us
    mul x1, local copies, waits for them, and re-layouts, per_device(): chosen = lesser * live_slots[None, :, None, :, None]  28.1 us
    all_to_all x1, blocking collectives, per_device(): lax.all_to_all(convolved, 'energy', split_axis=2, concat_axis=4, tiled=True)  23.1 us
    dot_general x12, matrix products, outer_part(): jnp.einsum('eckij,eckqj->cekiq', left_side, right_side, preferred_element...  22.3 us
    gather x2, local copies, waits for them, and re-layouts, toeplitz(): return jnp.take(screened, offsets, axis=2)  15.6 us
    dot_general x12, matrix products, strips(): jnp.einsum('ckp,ecpij->eckij', hot, shaped, preferred_element_type=jnp.fl...  12.3 us
    all_to_all x1, starting transfers between devices, per_device(): lax.all_to_all(chosen, 'energy', split_axis=4, concat_axis=2, tiled=True)  8.16 us
  transfers between devices with their start and end apart: 3, of which 1 were waited for; matrix products, arithmetic and copies ran while one was open for 15% of the time, Pallas kernels for 0%

commit v1 on v0

v1 whole, which is shorter than its diff:
```python
import jax
import jax.numpy as jnp
from jax import lax
from jax.experimental import pallas as pl
from jax.experimental.pallas import tpu as pltpu
from jax.sharding import PartitionSpec as P

ORB = 256
SUB = 64
KMAX = 8
LANES = 128
BF = jnp.bfloat16
F32 = jnp.float32


def mm(a, b):
    return jnp.dot(a, b, preferred_element_type=F32)


def mm_t(a, b):
    return lax.dot_general(a, b, (((1,), (1,)), ((), ())), preferred_element_type=F32)


def one_side(gr, gi, sr, si):
    inner_r = mm(jnp.concatenate([gr, -gi], 1), jnp.concatenate([sr, si], 0)).astype(BF)
    inner_i = mm(jnp.concatenate([gr, gi], 1), jnp.concatenate([si, sr], 0)).astype(BF)
    rows = []
    for b in range(ORB // SUB):
        part = slice(b * SUB, (b + 1) * SUB)
        rows.append(jnp.concatenate([gr[part], gi[part]], 1))
        rows.append(jnp.concatenate([-gi[part], gr[part]], 1))
    return mm_t(jnp.concatenate([inner_r, inner_i], 1), jnp.concatenate(rows, 0))


def lesser_cell(c, kept, count, g3, sx, l32, sel32, put):
    def energy(e, carry):
        total = one_side(g3[0][0, e, c], g3[0][1, e, c], sx[0, e, c + 1], sx[1, e, c + 1])
        total += one_side(g3[1][0, e, c], g3[1][1, e, c], sx[0, e, c], sx[1, e, c])
        total += one_side(g3[2][0, e, c], g3[2][1, e, c], sx[0, e, c + 2], sx[1, e, c + 2])
        for rb in range(ORB // SUB):
            for cb in range(ORB // SUB):
                l32[rb * 4 + cb] = total[rb * SUB : (rb + 1) * SUB, cb * LANES : (cb + 1) * LANES]
        live = count[c]
        for j in range(KMAX):
            sel32[j * 2 + e] = l32[kept[c, j]] * jnp.where(j < live, 1.0, 0.0).astype(F32)
        return carry

    lax.fori_loop(0, 2, energy, 0)
    low = lax.broadcasted_iota(jnp.int32, (16, LANES), 1) < SUB
    for d in range(32):
        even = sel32[:, 2 * d, :]
        odd = sel32[:, 2 * d + 1, :]
        put(d, 0, jnp.where(low, even, pltpu.roll(odd, SUB, 1)).astype(BF))
        put(d, 1, jnp.where(low, pltpu.roll(even, SUB, 1), odd).astype(BF))


def iota(shape, dim):
    return lax.broadcasted_iota(jnp.int32, shape, dim)


def build_kernels(screened, kmat):
    shape = (LANES, LANES)
    flip = (iota(shape, 0) == 126 - iota(shape, 1)).astype(BF)
    row, col = iota(shape, 0), iota(shape, 1)
    source = ((row // 2) % 2) * 64 + (row // 4) * 2 + row % 2
    row_pick = (source == col).astype(BF)
    wanted = (col // 64) * 64 + (col % 32) * 2 + (col // 32) % 2
    col_pick = (wanted == row).astype(BF)
    srow = iota((64, LANES), 0)
    low = iota((64, LANES), 1) < 64
    for c in range(4):
        halves = []
        for p in range(2):
            rev = mm(screened[p].astype(BF), flip)[c : c + 1]
            x = pltpu.roll(jnp.broadcast_to(rev, (64, LANES)), 65, 1)
            for bit in range(6):
                x = jnp.where((srow >> bit) % 2 == 1, pltpu.roll(x, 1 << bit, 1), x)
            halves.append(x)
        kr, ki = halves
        top = jnp.where(low, kr, pltpu.roll(-ki, 64, 1))
        bottom = jnp.where(low, ki, pltpu.roll(kr, 64, 1))
        natural = jnp.concatenate([top, bottom], 0).astype(BF)
        kmat[c] = mm(mm(row_pick, natural).astype(BF), col_pick).astype(BF)


def conv_cell(kc, get, x32, o32, put):
    x32[...] = get().astype(F32)
    for j in range(KMAX):
        parts = []
        for p in range(2):
            for e2 in range(2):
                parts.append(x32[:, p, 2 * j + e2, :].astype(BF))
        o32[:, j, :] = mm(kc, jnp.concatenate(parts, 0))
    put(o32[...].astype(BF))


def lesser_kernel(kept, count, gd, gl, gu, s, lo, hi, send, vd, vl, vu, sx, l32, sel32, sems):
    z = lax.axis_index("cell")
    last = lax.axis_size("cell") - 1
    copies = [
        pltpu.make_async_copy(gd, vd, sems.at[0]),
        pltpu.make_async_copy(gl, vl, sems.at[1]),
        pltpu.make_async_copy(gu, vu, sems.at[2]),
        pltpu.make_async_copy(s, sx.at[:, :, pl.ds(1, 4)], sems.at[3]),
        pltpu.make_async_copy(lo, sx.at[:, :, pl.ds(0, 1)], sems.at[4]),
        pltpu.make_async_copy(hi, sx.at[:, :, pl.ds(5, 1)], sems.at[5]),
    ]
    for copy in copies:
        copy.start()
    for copy in copies:
        copy.wait()

    def cell(c, carry):
        def put(d, p, value):
            send[d, c, p] = value

        lesser_cell(c, kept, count, (vd, vl, vu), sx, l32, sel32, put)
        return carry

    lax.fori_loop(0, 4, cell, 0)


def conv_kernel(screened, recv, send, kmat, x32, o32):
    build_kernels(screened, kmat)

    def cell(c, carry):
        def put(value):
            send[:, pl.ds(c, 1)] = value.reshape(32, 1, 4, KMAX, LANES)

        conv_cell(kmat[c], lambda: recv[:, c], x32, o32, put)
        return carry

    lax.fori_loop(0, 4, cell, 0)


def place_kernel(recv, out):
    def source(d, carry):
        for c in range(4):
            for pe in range(4):
                out[pe, c, :, pl.ds(pl.multiple_of(d * LANES, LANES), LANES)] = recv[d, c, pe]
        return carry

    lax.fori_loop(0, 32, source, 0)


VM = pl.BlockSpec(memory_space=pltpu.VMEM)
SM = pl.BlockSpec(memory_space=pltpu.SMEM)
ANY = pl.BlockSpec(memory_space=pl.ANY)


def per_device(gd, gl, gu, s, screened, kept, count):
    n = lax.axis_size("cell")
    lo = lax.ppermute(s[:, :, 3:4], "cell", [(i, i + 1) for i in range(n - 1)])
    hi = lax.ppermute(s[:, :, 0:1], "cell", [(i + 1, i) for i in range(n - 1)])
    limit = pltpu.CompilerParams(vmem_limit_bytes=60 * 1024 * 1024)
    big = pltpu.VMEM((2, 2, 4, ORB, ORB), BF)
    send = pl.pallas_call(
        lesser_kernel,
        out_shape=jax.ShapeDtypeStruct((32, 4, 2, 16, LANES), BF),
        in_specs=[SM, SM, ANY, ANY, ANY, ANY, ANY, ANY],
        out_specs=VM,
        scratch_shapes=[
            big,
            big,
            big,
            pltpu.VMEM((2, 2, 6, ORB, ORB), BF),
            pltpu.VMEM((16, SUB, LANES), F32),
            pltpu.VMEM((16, SUB, LANES), F32),
            pltpu.SemaphoreType.DMA((6,)),
        ],
        compiler_params=limit,
        name="lesser",
    )(kept, count, gd, gl, gu, s, lo, hi)
    recv = lax.all_to_all(send, "energy", split_axis=0, concat_axis=0, tiled=True)
    back = pl.pallas_call(
        conv_kernel,
        out_shape=jax.ShapeDtypeStruct((32, 4, 4, KMAX, LANES), BF),
        in_specs=[VM, VM],
        out_specs=VM,
        scratch_shapes=[
            pltpu.VMEM((4, LANES, LANES), BF),
            pltpu.VMEM((32, 2, 16, LANES), F32),
            pltpu.VMEM((LANES, KMAX, LANES), F32),
        ],
        compiler_params=limit,
        name="conv",
    )(screened, recv)
    got = lax.all_to_all(back, "energy", split_axis=0, concat_axis=0, tiled=True)
    out = pl.pallas_call(
        place_kernel,
        out_shape=jax.ShapeDtypeStruct((4, 4, KMAX, SUB * SUB), BF),
        in_specs=[VM],
        out_specs=VM,
        compiler_params=limit,
        name="place",
    )(got)
    return out.reshape(2, 2, 4, KMAX, SUB * SUB)


def solution(mesh):
    placed = P(None, "energy", "cell", None, None)
    return jax.shard_map(
        per_device,
        mesh=mesh,
        in_specs=(placed, placed, placed, placed, P(None, "cell", None), P("cell", None), P("cell")),
        out_specs=placed,
        check_vma=False,
    )
```

time: 211 us -> 95.5 us (0.45)
  local copies, waits for them, and re-layouts: 126 us -> 2.07 us
  matrix products: 42.3 us -> 0 us
  Pallas kernels: 0 us -> 28 us
  blocking collectives: 23.1 us -> 48.8 us
  waiting for transfers between devices: 1.01 us -> 8.75 us
  starting transfers between devices: 14 us -> 6.31 us
    unnamed x22 -> x4, local copies, waits for them, and re-layouts: 43.6 us -> 0.8 us
    dot_general x40 -> x0, matrix products: 42.3 us -> none  [the longest x12 22.3 us: outer_part(): jnp.einsum('eckij,eckqj->cekiq', left_side, right_side, preferred_element...]
    all_to_all x2 -> x0, local copies, waits for them, and re-layouts: 33.3 us -> none  [the longest x1 32.1 us: per_device(): lax.all_to_all(chosen, 'energy', split_axis=4, concat_axis=2, tiled=True)]
    mul x1 -> x0, local copies, waits for them, and re-layouts: 28.1 us -> none  [per_device(): chosen = lesser * live_slots[None, :, None, :, None]]
    pallas_call x0 -> x3, Pallas kernels: none -> 28 us  [the longest x1 16.1 us: per_device(): pl.pallas_call(lesser_kernel, out_shape=jax.ShapeDtypeStruct((32, 4, 2, 1...]
    all_to_all x1 -> x2, blocking collectives: 23.1 us -> 48.8 us  [the longest x1 27.4 us: per_device(): lax.all_to_all(send, 'energy', split_axis=0, concat_axis=0, tiled=True)]
    gather x2 -> x0, local copies, waits for them, and re-layouts: 15.6 us -> none  [toeplitz(): return jnp.take(screened, offsets, axis=2)]
    ppermute x2, waiting for transfers between devices: 0.01 us -> 8.75 us  [the longest x1 7.85 us: per_device(): hi = lax.ppermute(s[:, :, 0:1], 'cell', [(i + 1, i) for i in range(n - 1)])]
  transfers between devices with their start and end apart: 3 -> 2, of which waited for: 1 -> 2; matrix products, arithmetic and copies ran while one was open for 15% -> 0% of each run, Pallas kernels for 0% -> 0%
where the time goes in v1:
time: 95.5 us; the launch traced here: 94 us
  blocking collectives  48.8 us (51%)
  Pallas kernels  28 us (29%)
  waiting for transfers between devices  8.75 us (9%)
  starting transfers between devices  6.31 us (7%)
  local copies, waits for them, and re-layouts  2.07 us (2%)
    all_to_all x1, blocking collectives, per_device(): lax.all_to_all(send, 'energy', split_axis=0, concat_axis=0, tiled=True)  27.4 us
    all_to_all x1, blocking collectives, per_device(): lax.all_to_all(back, 'energy', split_axis=0, concat_axis=0, tiled=True)  21.4 us
    pallas_call x1, Pallas kernels, per_device(): pl.pallas_call(lesser_kernel, out_shape=jax.ShapeDtypeStruct((32, 4, 2, 1...  16.1 us
    pallas_call x1, Pallas kernels, per_device(): pl.pallas_call(conv_kernel, out_shape=jax.ShapeDtypeStruct((32, 4, 4, KMA...  9.42 us
    ppermute x1, waiting for transfers between devices, per_device(): hi = lax.ppermute(s[:, :, 0:1], 'cell', [(i + 1, i) for i in range(n - 1)])  7.85 us
    ppermute x1, starting transfers between devices, per_device(): lo = lax.ppermute(s[:, :, 3:4], 'cell', [(i, i + 1) for i in range(n - 1)])  5.02 us
    pallas_call x1, Pallas kernels, per_device(): pl.pallas_call(place_kernel, out_shape=jax.ShapeDtypeStruct((4, 4, KMAX,...  2.54 us
  transfers between devices with their start and end apart: 2, of which 2 were waited for; matrix products, arithmetic and copies ran while one was open for 0% of the time, Pallas kernels for 0%

profile of v1, /device:TPU:1, one launch (start us, length us, event | category | flops | bytes accessed | tf_op | source)
XLA Modules:
  0.0 94.0 jit_solution(17715306582811838001)
XLA Ops:
  0.0 1.3 %fusion = (bf16[2,2,1,256,256]{4,3,2,1,0:T(8,128)(2,1)S(1)}, bf16[2,2,1,256,256]{4,3,2,1,0:T(8,128)(2,1)S(1)}) fusion(bf16[2,2,4,256,256]{4,3,2,1,0:T(8,128)(2,1)} %s.1), kind=kLoop, calls=%fused_computation | loop fusion | bytes 2097152 | tf_op jit(solution)/shard_map/slice | solution.py:154
  1.3 1.3 %collective-permute-start.1 = (bf16[2,2,1,256,256]{4,3,2,1,0:T(8,128)(2,1)S(1)}, bf16[2,2,1,256,256]{4,3,2,1,0:T(8,128)(2,1)S(1)}, u32[]{:S(2)}, u32[]{:S(2)}) collective-permute-start(bf16[2,2,1,256,256]{4,3,2,1,0:T(8,128)(2,1)S(1)} %get-tuple-element.5), channel_id=1, source_target_pairs={{1,0},{2,1},{3,2},{4,3},{5,4},{6,5},{7,6},{9,8},{10,9},{11,10},{12... | collective-permute-start | bytes 1572872 | tf_op jit(solution)/shard_map/ppermute | solution.py:154
  2.6 5.0 %collective-permute-start = (bf16[2,2,1,256,256]{4,3,2,1,0:T(8,128)(2,1)S(1)}, bf16[2,2,1,256,256]{4,3,2,1,0:T(8,128)(2,1)S(1)}, u32[]{:S(2)}, u32[]{:S(2)}) collective-permute-start(bf16[2,2,1,256,256]{4,3,2,1,0:T(8,128)(2,1)S(1)} %get-tuple-element.6), channel_id=1, source_target_pairs={{0,1},{1,2},{2,3},{3,4},{4,5},{5,6},{6,7},{8,9},{9,10},{10,11},{11... | collective-permute-start | bytes 1572872 | tf_op jit(solution)/shard_map/ppermute | solution.py:153
  7.6 7.8 %collective-permute-done.1.hi = bf16[2,2,1,256,256]{4,3,2,1,0:T(8,128)(2,1)S(1)} collective-permute-done((bf16[2,2,1,256,256]{4,3,2,1,0:T(8,128)(2,1)S(1)}, bf16[2,2,1,256,256]{4,3,2,1,0:T(8,128)(2,1)S(1)}, u32[]{:S(2)}, u32[]{:S(2)}) %collective-permute-start.1) | collective-permute-done | bytes 524320 | tf_op jit(solution)/shard_map/ppermute | solution.py:154
  15.5 0.0 copy-start
  15.5 0.9 collective-permute-done.lo
  16.4 0.0 copy-done
  16.4 0.0 copy-start.1
  16.4 0.8 copy-done.1
  17.2 16.1 %lesser.1 = bf16[32,4,2,16,128]{4,3,2,1,0:T(8,128)(2,1)} custom-call(s32[4,8]{1,0:T(4,128)} %kept.1, s32[4]{0:T(128)} %count.1, bf16[2,2,4,256,256]{4,3,2,1,0:T(8,128)(2,1)} %gd.1, bf16[2,2,4,256,256]{4,3,2,1,0:T(8,128)(2,1)} %gl.1, bf16[2,2,4,256,256]{4,3,2,1,0:T(8,128)(2,1)} %gu.1, bf16[2,2,4,256,256]{4,3,2,1,0:T(8,128)(2,1)} %s.1, ...), custom_call_target="tpu_custom_call" | custom-call | tf_op jit(solution)/shard_map/lesser/pallas_call | solution.py:157
  33.2 27.4 %all_to_all.10.recv = bf16[32,4,2,16,128]{4,3,2,1,0:T(8,128)(2,1)} all-to-all(bf16[32,4,2,16,128]{4,3,2,1,0:T(8,128)(2,1)} %lesser.1), channel_id=1, replica_groups=mesh['energy'=32,'cell'=8] {'energy'}, dimensions={0} | all-to-all | bytes 2097152 | tf_op jit(solution)/shard_map/all_to_all | solution.py:174
  60.7 9.4 %conv.1 = bf16[32,4,4,8,128]{4,3,2,1,0:T(8,128)(2,1)} custom-call(bf16[2,4,128]{2,1,0:T(4,128)(2,1)} %screened.1, bf16[32,4,2,16,128]{4,3,2,1,0:T(8,128)(2,1)} %all_to_all.10.recv), custom_call_target="tpu_custom_call" | custom-call | tf_op jit(solution)/shard_map/conv/pallas_call | solution.py:175
  70.1 21.4 %all_to_all.11.recv = bf16[32,4,4,8,128]{4,3,2,1,0:T(8,128)(2,1)} all-to-all(bf16[32,4,4,8,128]{4,3,2,1,0:T(8,128)(2,1)} %conv.1), channel_id=1, replica_groups=mesh['energy'=32,'cell'=8] {'energy'}, dimensions={0} | all-to-all | bytes 2097152 | tf_op jit(solution)/shard_map/all_to_all | solution.py:188
  91.5 2.5 %place.1 = bf16[4,4,8,4096]{3,2,1,0:T(8,128)(2,1)} custom-call(bf16[32,4,4,8,128]{4,3,2,1,0:T(8,128)(2,1)} %all_to_all.11.recv), custom_call_target="tpu_custom_call" | custom-call | tf_op jit(solution)/shard_map/place/pallas_call | solution.py:189
Async XLA Ops:
  1.3 14.2 %collective-permute-start.1 = (bf16[2,2,1,256,256]{4,3,2,1,0:T(8,128)(2,1)S(1)}, bf16[2,2,1,256,256]{4,3,2,1,0:T(8,128)(2,1)S(1)}, u32[]{:S(2)}, u32[]{:S(2)}) collective-permute-start(bf16[2,2,1,256,256]{4,3,2,1,0:T(8,128)(2,1)S(1)} %get-tuple-element.5), channel_id=1, source_target_pairs={{1,0},{2,1},{3,2},{4,3},{5,4},{6,5},{7,6},{9,8},{10,9},{11,10},{12... | collective-permute-start | bytes 1572872 | tf_op jit(solution)/shard_map/ppermute | solution.py:154
  2.6 13.8 %collective-permute-start = (bf16[2,2,1,256,256]{4,3,2,1,0:T(8,128)(2,1)S(1)}, bf16[2,2,1,256,256]{4,3,2,1,0:T(8,128)(2,1)S(1)}, u32[]{:S(2)}, u32[]{:S(2)}) collective-permute-start(bf16[2,2,1,256,256]{4,3,2,1,0:T(8,128)(2,1)S(1)} %get-tuple-element.6), channel_id=1, source_target_pairs={{0,1},{1,2},{2,3},{3,4},{4,5},{5,6},{6,7},{8,9},{9,10},{10,11},{11... | collective-permute-start | bytes 1572872 | tf_op jit(solution)/shard_map/ppermute | solution.py:153
  15.5 0.9 copy-start
  16.4 0.8 copy-start.1

commit v2 on v1

--- a/solution.py
+++ b/solution.py
@@ -94,71 +94,141 @@
     put(o32[...].astype(BF))
 
 
-def lesser_kernel(kept, count, gd, gl, gu, s, lo, hi, send, vd, vl, vu, sx, l32, sel32, sems):
+def whole(kept, count, screened, gd, gl, gu, s, out, vd, vl, vu, sx, l32, sel32, send_a, recv_a, kmat, x32, o32, send_b,
+          in_sem, s_sem, halo_send, halo_recv, a_send, a_recv, b_send, b_recv):
+    me = lax.axis_index("energy")
     z = lax.axis_index("cell")
-    last = lax.axis_size("cell") - 1
-    copies = [
-        pltpu.make_async_copy(gd, vd, sems.at[0]),
-        pltpu.make_async_copy(gl, vl, sems.at[1]),
-        pltpu.make_async_copy(gu, vu, sems.at[2]),
-        pltpu.make_async_copy(s, sx.at[:, :, pl.ds(1, 4)], sems.at[3]),
-        pltpu.make_async_copy(lo, sx.at[:, :, pl.ds(0, 1)], sems.at[4]),
-        pltpu.make_async_copy(hi, sx.at[:, :, pl.ds(5, 1)], sems.at[5]),
+    up = lax.rem(z + 1, 8)
+    down = lax.rem(z + 7, 8)
+    own = pltpu.make_async_copy(s, sx.at[:, :, pl.ds(1, 4)], s_sem)
+    own.start()
+
+    def inputs(c):
+        here = pl.ds(c, 1)
+        return [
+            pltpu.make_async_copy(g.at[:, :, here], v.at[:, :, here], in_sem.at[c, k])
+            for k, (g, v) in enumerate(((gd, vd), (gl, vl), (gu, vu)))
+        ]
+
+    for c in (1, 2, 0, 3):
+        for copy in inputs(c):
+            copy.start()
+
+    barrier = pltpu.get_barrier_semaphore()
+
+    def greet(k, carry):
+        pl.semaphore_signal(barrier, 1, device_id=(lax.rem(me + k, 32), z), device_id_type=MESH)
+        return carry
+
+    lax.fori_loop(1, 32, greet, 0)
+    pl.semaphore_signal(barrier, 1, device_id=(me, up), device_id_type=MESH)
+    pl.semaphore_signal(barrier, 1, device_id=(me, down), device_id_type=MESH)
+    pl.semaphore_wait(barrier, 33)
+
+    halos = [
+        pltpu.make_async_remote_copy(
+            s.at[:, :, pl.ds(source, 1)], sx.at[:, :, pl.ds(target, 1)], halo_send.at[k], halo_recv.at[k],
+            device_id=(me, where), device_id_type=MESH,
+        )
+        for k, (source, target, where) in enumerate(((3, 0, up), (0, 5, down)))
     ]
-    for copy in copies:
-        copy.start()
-    for copy in copies:
-        copy.wait()
-
-    def cell(c, carry):
+    for halo in halos:
+        halo.start()
+    own.wait()
+
+    def lesser(c):
+        for copy in inputs(c):
+            copy.wait()
+
         def put(d, p, value):
-            send[d, c, p] = value
+            send_a[c, d, p] = value
 
         lesser_cell(c, kept, count, (vd, vl, vu), sx, l32, sel32, put)
-        return carry
-
-    lax.fori_loop(0, 4, cell, 0)
-
-
-def conv_kernel(screened, recv, send, kmat, x32, o32):
-    build_kernels(screened, kmat)
-
-    def cell(c, carry):
+        pltpu.make_async_copy(send_a.at[c, me], recv_a.at[c, me], a_recv.at[c]).start()
+
+        def push(k, carry):
+            to = lax.rem(me + k, 32)
+            pltpu.make_async_remote_copy(
+                send_a.at[c, to], recv_a.at[c, me], a_send.at[c], a_recv.at[c],
+                device_id=(to, z), device_id_type=MESH,
+            ).start()
+            return carry
+
+        lax.fori_loop(1, 32, push, 0)
+
+    def convolve(c):
+        pltpu.make_async_copy(recv_a.at[c], recv_a.at[c], a_recv.at[c]).wait()
+
         def put(value):
-            send[:, pl.ds(c, 1)] = value.reshape(32, 1, 4, KMAX, LANES)
-
-        conv_cell(kmat[c], lambda: recv[:, c], x32, o32, put)
-        return carry
-
-    lax.fori_loop(0, 4, cell, 0)
-
-
-def place_kernel(recv, out):
-    def source(d, carry):
-        for c in range(4):
-            for pe in range(4):
-                out[pe, c, :, pl.ds(pl.multiple_of(d * LANES, LANES), LANES)] = recv[d, c, pe]
-        return carry
-
-    lax.fori_loop(0, 32, source, 0)
+            send_b[c] = value.reshape(32, 4, KMAX, LANES)
+
+        conv_cell(kmat[c], lambda: recv_a[c], x32, o32, put)
+        mine = pl.ds(pl.multiple_of(me * LANES, LANES), LANES)
+        pltpu.make_async_copy(send_b.at[c, me], out.at[:, c, :, mine], b_recv.at[c]).start()
+
+        def push(k, carry):
+            to = lax.rem(me + k, 32)
+            pltpu.make_async_remote_copy(
+                send_b.at[c, to], out.at[:, c, :, mine], b_send.at[c], b_recv.at[c],
+                device_id=(to, z), device_id_type=MESH,
+            ).start()
+            return carry
+
+        lax.fori_loop(1, 32, push, 0)
+
+    def halves(h, carry):
+        @pl.when(h == 1)
+        def _():
+            for halo in halos:
+                halo.wait()
+
+            @pl.when(z == 0)
+            def _():
+                sx[:, :, 0] = jnp.zeros((2, 2, ORB, ORB), BF)
+
+            @pl.when(z == 7)
+            def _():
+                sx[:, :, 5] = jnp.zeros((2, 2, ORB, ORB), BF)
+
+        def first(i, carry):
+            lesser(jnp.where(h == 0, 1 + i, 3 * i))
+            return carry
+
+        lax.fori_loop(0, 2, first, 0)
+
+        @pl.when(h == 0)
+        def _():
+            build_kernels(screened, kmat)
+
+        def second(i, carry):
+            convolve(jnp.where(h == 0, 1 + i, 3 * i))
+            return carry
+
+        return lax.fori_loop(0, 2, second, carry)
+
+    lax.fori_loop(0, 2, halves, 0)
+    for c in range(4):
+        pltpu.make_async_copy(out.at[:, c], out.at[:, c], b_recv.at[c]).wait()
+        sent = send_a.at[c, pl.ds(0, 31)]
+        pltpu.make_async_copy(sent, sent, a_send.at[c]).wait()
+        sent = send_b.at[c, pl.ds(0, 31)]
+        pltpu.make_async_copy(sent, sent, b_send.at[c]).wait()
 
 
 VM = pl.BlockSpec(memory_space=pltpu.VMEM)
 SM = pl.BlockSpec(memory_space=pltpu.SMEM)
 ANY = pl.BlockSpec(memory_space=pl.ANY)
+MESH = pl.DeviceIdType.MESH
 
 
 def per_device(gd, gl, gu, s, screened, kept, count):
-    n = lax.axis_size("cell")
-    lo = lax.ppermute(s[:, :, 3:4], "cell", [(i, i + 1) for i in range(n - 1)])
-    hi = lax.ppermute(s[:, :, 0:1], "cell", [(i + 1, i) for i in range(n - 1)])
-    limit = pltpu.CompilerParams(vmem_limit_bytes=60 * 1024 * 1024)
     big = pltpu.VMEM((2, 2, 4, ORB, ORB), BF)
-    send = pl.pallas_call(
-        lesser_kernel,
-        out_shape=jax.ShapeDtypeStruct((32, 4, 2, 16, LANES), BF),
-        in_specs=[SM, SM, ANY, ANY, ANY, ANY, ANY, ANY],
-        out_specs=VM,
+    dma = pltpu.SemaphoreType.DMA
+    out = pl.pallas_call(
+        whole,
+        out_shape=jax.ShapeDtypeStruct((4, 4, KMAX, SUB * SUB), BF),
+        in_specs=[SM, SM, VM, ANY, ANY, ANY, ANY],
+        out_specs=ANY,
         scratch_shapes=[
             big,
             big,
@@ -166,34 +236,26 @@
             pltpu.VMEM((2, 2, 6, ORB, ORB), BF),
             pltpu.VMEM((16, SUB, LANES), F32),
             pltpu.VMEM((16, SUB, LANES), F32),
-            pltpu.SemaphoreType.DMA((6,)),
-        ],
-        compiler_params=limit,
-        name="lesser",
-    )(kept, count, gd, gl, gu, s, lo, hi)
-    recv = lax.all_to_all(send, "energy", split_axis=0, concat_axis=0, tiled=True)
-    back = pl.pallas_call(
-        conv_kernel,
-        out_shape=jax.ShapeDtypeStruct((32, 4, 4, KMAX, LANES), BF),
-        in_specs=[VM, VM],
-        out_specs=VM,
-        scratch_shapes=[
+            pltpu.VMEM((4, 32, 2, 16, LANES), BF),
+            pltpu.VMEM((4, 32, 2, 16, LANES), BF),
             pltpu.VMEM((4, LANES, LANES), BF),
             pltpu.VMEM((32, 2, 16, LANES), F32),
             pltpu.VMEM((LANES, KMAX, LANES), F32),
+            pltpu.VMEM((4, 32, 4, KMAX, LANES), BF),
+            dma((4, 3)),
+            dma(()),
+            dma((2,)),
+            dma((2,)),
+            dma((4,)),
+            dma((4,)),
+            dma((4,)),
+            dma((4,)),
         ],
-        compiler_params=limit,
-        name="conv",
-    )(screened, recv)
-    got = lax.all_to_all(back, "energy", split_axis=0, concat_axis=0, tiled=True)
-    out = pl.pallas_call(
-        place_kernel,
-        out_shape=jax.ShapeDtypeStruct((4, 4, KMAX, SUB * SUB), BF),
-        in_specs=[VM],
-        out_specs=VM,
-        compiler_params=limit,
-        name="place",
-    )(got)
+        compiler_params=pltpu.CompilerParams(
+            vmem_limit_bytes=60 * 1024 * 1024, collective_id=0, has_side_effects=True
+        ),
+        name="whole",
+    )(kept, count, screened, gd, gl, gu, s)
     return out.reshape(2, 2, 4, KMAX, SUB * SUB)
 
 

time: 95.5 us -> 47.8 us (0.50); the launches traced: 94 us -> 47.7 us
  blocking collectives: 48.8 us -> 0 us
  Pallas kernels: 28 us -> 45.4 us
  waiting for transfers between devices: 8.75 us -> 0 us
  starting transfers between devices: 6.31 us -> 0 us
    all_to_all x2 -> x0, blocking collectives: 48.8 us -> none  [the longest x1 27.4 us: per_device(): lax.all_to_all(send, 'energy', split_axis=0, concat_axis=0, tiled=True)]
    pallas_call x3 -> x1, Pallas kernels: 28 us -> 45.4 us  [per_device(): pl.pallas_call(whole, out_shape=jax.ShapeDtypeStruct((4, 4, KMAX, SUB * S...]
    ppermute x2 -> x0, waiting for transfers between devices: 8.75 us -> none  [the longest x1 7.85 us: per_device(): hi = lax.ppermute(s[:, :, 0:1], 'cell', [(i + 1, i) for i in range(n - 1)])]
    ppermute x2 -> x0, starting transfers between devices: 6.31 us -> none  [the longest x1 5.02 us: per_device(): lo = lax.ppermute(s[:, :, 3:4], 'cell', [(i, i + 1) for i in range(n - 1)])]
    unnamed x4 -> x1, local copies, waits for them, and re-layouts: 0.8 us -> 2.29 us
    slice x1 -> x0, local copies, waits for them, and re-layouts: 1.27 us -> none  [per_device(): hi = lax.ppermute(s[:, :, 0:1], 'cell', [(i + 1, i) for i in range(n - 1)])]
  transfers between devices with their start and end apart: 2 -> 0, of which waited for: 2 -> 0; matrix products, arithmetic and copies ran while one was open for 0% -> 0% of each run, Pallas kernels for 0% -> 0%
where the time goes in v2:
time: 47.8 us; the launch traced here: 47.7 us
  Pallas kernels  45.4 us (95%)
  local copies, waits for them, and re-layouts  2.29 us (5%)
    pallas_call x1, Pallas kernels, per_device(): pl.pallas_call(whole, out_shape=jax.ShapeDtypeStruct((4, 4, KMAX, SUB * S...  45.4 us
    unnamed x1, local copies, waits for them, and re-layouts  2.29 us

profile of v2, /device:TPU:1, one launch (start us, length us, event | category | flops | bytes accessed | tf_op | source)
XLA Modules:
  0.0 47.7 jit_solution(4493308365684010300)
XLA Ops:
  0.0 45.4 %whole.1 = bf16[4,4,8,4096]{3,2,1,0:T(8,128)(2,1)} custom-call(s32[4,8]{1,0:T(4,128)} %kept.1, s32[4]{0:T(128)} %count.1, bf16[2,4,128]{2,1,0:T(4,128)(2,1)} %screened.1, bf16[2,2,4,256,256]{4,3,2,1,0:T(8,128)(2,1)} %gd.1, bf16[2,2,4,256,256]{4,3,2,1,0:T(8,128)(2,1)} %gl.1, bf16[2,2,4,256,256]{4,3,2,1,0:T(8,128)(2,1)} %gu.1, bf16[2,2,4,256,256]{4,3,2,1,0:T(8,128)(2,1)} %s.1), custom_call_target="tpu_custom_call" | custom-call | tf_op jit(solution)/shard_map/whole/pallas_call | solution.py:227
  45.4 2.3 %copy.9 = bf16[2,2,4,8,4096]{4,3,2,1,0:T(8,128)(2,1)} copy(bf16[2,2,4,8,4096]{4,3,2,1,0:T(8,128)(2,1)} %bitcast.1) | data formatting | bytes 2097152

commit v3 on v2

v3 whole, which is shorter than its diff:
```python
import jax
import jax.numpy as jnp
from jax import lax
from jax.experimental import pallas as pl
from jax.experimental.pallas import tpu as pltpu
from jax.sharding import PartitionSpec as P

ORB = 256
SUB = 64
KMAX = 8
LANES = 128
BF = jnp.bfloat16
F32 = jnp.float32


def mm(a, b):
    return jnp.dot(a, b, preferred_element_type=F32)


def mm_t(a, b):
    return lax.dot_general(a, b, (((1,), (1,)), ((), ())), preferred_element_type=F32)


def one_side(gr, gi, sr, si):
    inner_r = mm(jnp.concatenate([gr, -gi], 1), jnp.concatenate([sr, si], 0)).astype(BF)
    inner_i = mm(jnp.concatenate([gr, gi], 1), jnp.concatenate([si, sr], 0)).astype(BF)
    rows = []
    for b in range(ORB // SUB):
        part = slice(b * SUB, (b + 1) * SUB)
        rows.append(jnp.concatenate([gr[part], gi[part]], 1))
        rows.append(jnp.concatenate([-gi[part], gr[part]], 1))
    return mm_t(jnp.concatenate([inner_r, inner_i], 1), jnp.concatenate(rows, 0))


def side(c, e, k, at, vg, sx):
    return one_side(vg[k, 0, e, c], vg[k, 1, e, c], sx[0, e, at], sx[1, e, at])


def store_blocks(total, part):
    for rb in range(ORB // SUB):
        for cb in range(ORB // SUB):
            part[rb * 4 + cb] = total[rb * SUB : (rb + 1) * SUB, cb * LANES : (cb + 1) * LANES]


def select(c, e, kept, count, part, sel32):
    live = count[c]
    for j in range(KMAX):
        rows = pl.ds(pl.multiple_of((j * 2 + e) * SUB, SUB), SUB)
        sel32[rows, :] = part[kept[c, j]] * jnp.where(j < live, 1.0, 0.0).astype(F32)


def pack(sel32, put):
    low = iota((16, LANES), 1) < SUB
    for d in range(32):
        even = sel32[pl.ds(2 * d, 16, stride=SUB), :]
        odd = sel32[pl.ds(2 * d + 1, 16, stride=SUB), :]
        put(d, 0, jnp.where(low, even, pltpu.roll(odd, SUB, 1)).astype(BF))
        put(d, 1, jnp.where(low, pltpu.roll(even, SUB, 1), odd).astype(BF))


def iota(shape, dim):
    return lax.broadcasted_iota(jnp.int32, shape, dim)


def build_kernels(screened, kmat):
    shape = (LANES, LANES)
    flip = (iota(shape, 0) == 126 - iota(shape, 1)).astype(BF)
    row, col = iota(shape, 0), iota(shape, 1)
    source = ((row // 2) % 2) * 64 + (row // 4) * 2 + row % 2
    row_pick = (source == col).astype(BF)
    wanted = (col // 64) * 64 + (col % 32) * 2 + (col // 32) % 2
    col_pick = (wanted == row).astype(BF)
    srow = iota((256, LANES), 0)
    low = iota((64, LANES), 1) < 64
    rev = mm(jnp.concatenate([screened[0], screened[1]], 0), flip)
    halves = []
    for p in range(2):
        rows = [jnp.broadcast_to(rev[4 * p + c : 4 * p + c + 1], (64, LANES)) for c in range(4)]
        x = pltpu.roll(jnp.concatenate(rows, 0), 65, 1)
        for bit in range(6):
            x = jnp.where((srow >> bit) % 2 == 1, pltpu.roll(x, 1 << bit, 1), x)
        halves.append(x)
    natural = []
    for c in range(4):
        kr, ki = (half[c * 64 : c * 64 + 64] for half in halves)
        top = jnp.where(low, kr, pltpu.roll(-ki, 64, 1))
        bottom = jnp.where(low, ki, pltpu.roll(kr, 64, 1))
        natural.append(jnp.concatenate([top, bottom], 0).astype(BF))
    picked = mm(row_pick, jnp.concatenate(natural, 1)).astype(BF)
    stacked = jnp.concatenate([picked[:, c * LANES : (c + 1) * LANES] for c in range(4)], 0)
    done = mm(stacked, col_pick).astype(BF)
    for c in range(4):
        kmat[c] = done[c * LANES : (c + 1) * LANES]


def conv_cell(kc, get, x32, o32, put):
    x32[...] = get().astype(F32).reshape(1024, LANES)
    for j in range(KMAX):
        parts = []
        for p in range(2):
            for e2 in range(2):
                parts.append(x32[pl.ds(p * 16 + 2 * j + e2, 32, stride=32), :].astype(BF))
        o32[pl.ds(j, LANES, stride=KMAX), :] = mm(kc, jnp.concatenate(parts, 0))
    put(o32[...].astype(BF))


def whole(kept, count, screened, gd, gl, gu, s, out, vg, sx, part, sel32, send_a, recv_a, kmat, x32, o32, send_b,
          in_sem, s_sem, halo_send, halo_recv, a_send, a_recv, b_send, b_recv):
    me = lax.axis_index("energy")
    z = lax.axis_index("cell")
    up = lax.rem(z + 1, 8)
    down = lax.rem(z + 7, 8)

    def inputs(c):
        here = pl.ds(c, 1)
        return [
            pltpu.make_async_copy(g.at[:, :, here], vg.at[k, :, :, here], in_sem.at[c, k])
            for k, g in enumerate((gd, gl, gu))
        ]

    own = pltpu.make_async_copy(s, sx.at[:, :, pl.ds(1, 4)], s_sem)
    own.start()
    for c in (1, 2, 0, 3):
        for copy in inputs(c):
            copy.start()

    barrier = pltpu.get_barrier_semaphore()
    pl.semaphore_signal(barrier, 1, device_id=(me, up), device_id_type=MESH)
    pl.semaphore_signal(barrier, 1, device_id=(me, down), device_id_type=MESH)

    def greet(k, carry):
        pl.semaphore_signal(barrier, 1, device_id=(lax.rem(me + k, 32), z), device_id_type=MESH)
        return carry

    lax.fori_loop(1, 32, greet, 0)
    build_kernels(screened, kmat)
    pl.semaphore_wait(barrier, 33)

    halos = [
        pltpu.make_async_remote_copy(
            s.at[:, :, pl.ds(source, 1)], sx.at[:, :, pl.ds(target, 1)], halo_send.at[k], halo_recv.at[k],
            device_id=(me, where), device_id_type=MESH,
        )
        for k, (source, target, where) in enumerate(((3, 0, up), (0, 5, down)))
    ]
    for halo in halos:
        halo.start()
    own.wait()

    def send_cell(c):
        def put(d, p, value):
            send_a[c, d, p] = value

        pack(sel32, put)
        pltpu.make_async_copy(send_a.at[c, me], recv_a.at[c, me], a_recv.at[c]).start()

        def push(k, carry):
            to = lax.rem(me + k, 32)
            pltpu.make_async_remote_copy(
                send_a.at[c, to], recv_a.at[c, me], a_send.at[c], a_recv.at[c],
                device_id=(to, z), device_id_type=MESH,
            ).start()
            return carry

        lax.fori_loop(1, 32, push, 0)

    def convolve(c):
        pltpu.make_async_copy(recv_a.at[c], recv_a.at[c], a_recv.at[c]).wait()

        def put(value):
            send_b[c] = value.reshape(32, 4, KMAX, LANES)

        conv_cell(kmat[c], lambda: recv_a[c], x32, o32, put)
        mine = pl.ds(pl.multiple_of(me * LANES, LANES), LANES)
        pltpu.make_async_copy(send_b.at[c, me], out.at[:, c, :, mine], b_recv.at[c]).start()

        def push(k, carry):
            to = lax.rem(me + k, 32)
            pltpu.make_async_remote_copy(
                send_b.at[c, to], out.at[:, c, :, mine], b_send.at[c], b_recv.at[c],
                device_id=(to, z), device_id_type=MESH,
            ).start()
            return carry

        lax.fori_loop(1, 32, push, 0)

    def inner_cell(i, carry):
        c = 1 + i
        for copy in inputs(c):
            copy.wait()

        def energy(e, carry):
            total = side(c, e, 0, c + 1, vg, sx) + side(c, e, 1, c, vg, sx) + side(c, e, 2, c + 2, vg, sx)
            store_blocks(total, part.at[0, e])
            select(c, e, kept, count, part.at[0, e], sel32)
            return carry

        lax.fori_loop(0, 2, energy, 0)
        send_cell(c)
        return carry

    def edge_start(i, carry):
        c = 3 * i
        for copy in inputs(c):
            copy.wait()

        def energy(e, carry):
            store_blocks(side(c, e, 0, c + 1, vg, sx) + side(c, e, 2 - i, 2 + i, vg, sx), part.at[i, e])
            return carry

        lax.fori_loop(0, 2, energy, 0)
        convolve(1 + i)
        return carry

    def edge_end(i, carry):
        c = 3 * i
        inside = jnp.where(z == 7 * i, 0.0, 1.0).astype(BF)

        def energy(e, carry):
            at = 5 * i
            total = one_side(vg[1 + i, 0, e, c], vg[1 + i, 1, e, c], sx[0, e, at] * inside, sx[1, e, at] * inside)
            for rb in range(ORB // SUB):
                for cb in range(ORB // SUB):
                    block = total[rb * SUB : (rb + 1) * SUB, cb * LANES : (cb + 1) * LANES]
                    part[i, e, rb * 4 + cb] += block
            select(c, e, kept, count, part.at[i, e], sel32)
            return carry

        lax.fori_loop(0, 2, energy, 0)
        send_cell(c)
        return carry

    def edge_convolve(i, carry):
        convolve(3 * i)
        return carry

    lax.fori_loop(0, 2, inner_cell, 0)
    lax.fori_loop(0, 2, edge_start, 0)
    for halo in halos:
        halo.wait()
    lax.fori_loop(0, 2, edge_end, 0)
    lax.fori_loop(0, 2, edge_convolve, 0)
    for c in range(4):
        pltpu.make_async_copy(out.at[:, c], out.at[:, c], b_recv.at[c]).wait()
        sent = send_a.at[c, pl.ds(0, 31)]
        pltpu.make_async_copy(sent, sent, a_send.at[c]).wait()
        sent = send_b.at[c, pl.ds(0, 31)]
        pltpu.make_async_copy(sent, sent, b_send.at[c]).wait()


VM = pl.BlockSpec(memory_space=pltpu.VMEM)
SM = pl.BlockSpec(memory_space=pltpu.SMEM)
ANY = pl.BlockSpec(memory_space=pl.ANY)
MESH = pl.DeviceIdType.MESH


def per_device(gd, gl, gu, s, screened, kept, count):
    dma = pltpu.SemaphoreType.DMA
    out = pl.pallas_call(
        whole,
        out_shape=pltpu.VMEM((4, 4, KMAX, SUB * SUB), BF),
        in_specs=[SM, SM, VM, ANY, ANY, ANY, ANY],
        out_specs=VM,
        scratch_shapes=[
            pltpu.VMEM((3, 2, 2, 4, ORB, ORB), BF),
            pltpu.VMEM((2, 2, 6, ORB, ORB), BF),
            pltpu.VMEM((2, 2, 16, SUB, LANES), F32),
            pltpu.VMEM((16 * SUB, LANES), F32),
            pltpu.VMEM((4, 32, 2, 16, LANES), BF),
            pltpu.VMEM((4, 32, 2, 16, LANES), BF),
            pltpu.VMEM((4, LANES, LANES), BF),
            pltpu.VMEM((32 * 32, LANES), F32),
            pltpu.VMEM((LANES * KMAX, LANES), F32),
            pltpu.VMEM((4, 32, 4, KMAX, LANES), BF),
            dma((4, 3)),
            dma(()),
            dma((2,)),
            dma((2,)),
            dma((4,)),
            dma((4,)),
            dma((4,)),
            dma((4,)),
        ],
        compiler_params=pltpu.CompilerParams(
            vmem_limit_bytes=60 * 1024 * 1024, collective_id=0, has_side_effects=True
        ),
        name="whole",
    )(kept, count, screened, gd, gl, gu, s)
    return out.reshape(2, 2, 4, KMAX, SUB * SUB)


def solution(mesh):
    placed = P(None, "energy", "cell", None, None)
    return jax.shard_map(
        per_device,
        mesh=mesh,
        in_specs=(placed, placed, placed, placed, P(None, "cell", None), P("cell", None), P("cell")),
        out_specs=placed,
        check_vma=False,
    )
```

time: 47.8 us -> 45.3 us (0.948)
  local copies, waits for them, and re-layouts: 2.29 us -> 0.97 us
  Pallas kernels: 45.4 us -> 44.2 us
    unnamed x1, local copies, waits for them, and re-layouts: 2.29 us -> 0.97 us
    pallas_call x1, Pallas kernels: 45.4 us -> 44.2 us  [per_device(): pl.pallas_call(whole, out_shape=pltpu.VMEM((4, 4, KMAX, SUB * SUB), BF),...]
where the time goes in v3:
time: 45.3 us; the launch traced here: 45.1 us
  Pallas kernels  44.2 us (98%)
  local copies, waits for them, and re-layouts  0.97 us (2%)
    pallas_call x1, Pallas kernels, per_device(): pl.pallas_call(whole, out_shape=pltpu.VMEM((4, 4, KMAX, SUB * SUB), BF),...  44.2 us
    unnamed x1, local copies, waits for them, and re-layouts  0.97 us

profile of v3, /device:TPU:1, one launch (start us, length us, event | category | flops | bytes accessed | tf_op | source)
XLA Modules:
  0.0 45.1 jit_solution(13621941249247626817)
XLA Ops:
  0.0 44.2 %whole.1 = bf16[4,4,8,4096]{3,2,1,0:T(8,128)(2,1)S(1)} custom-call(s32[4,8]{1,0:T(4,128)} %kept.1, s32[4]{0:T(128)} %count.1, bf16[2,4,128]{2,1,0:T(4,128)(2,1)} %screened.1, bf16[2,2,4,256,256]{4,3,2,1,0:T(8,128)(2,1)} %gd.1, bf16[2,2,4,256,256]{4,3,2,1,0:T(8,128)(2,1)} %gl.1, bf16[2,2,4,256,256]{4,3,2,1,0:T(8,128)(2,1)} %gu.1, bf16[2,2,4,256,256]{4,3,2,1,0:T(8,128)(2,1)} %s.1), custom_call_target="tpu_custom_call" | custom-call | tf_op jit(solution)/shard_map/whole/pallas_call | solution.py:259
  44.2 1.0 %copy.9 = bf16[2,2,4,8,4096]{4,3,2,1,0:T(8,128)(2,1)} copy(bf16[2,2,4,8,4096]{4,3,2,1,0:T(8,128)(2,1)S(1)} %bitcast.1) | data formatting | bytes 2097152

commit v4 on v3

--- a/solution.py
+++ b/solution.py
@@ -45,17 +45,17 @@
 def select(c, e, kept, count, part, sel32):
     live = count[c]
     for j in range(KMAX):
-        rows = pl.ds(pl.multiple_of((j * 2 + e) * SUB, SUB), SUB)
+        rows = pl.ds(pl.multiple_of((e * KMAX + j) * SUB, SUB), SUB)
         sel32[rows, :] = part[kept[c, j]] * jnp.where(j < live, 1.0, 0.0).astype(F32)
 
 
-def pack(sel32, put):
-    low = iota((16, LANES), 1) < SUB
+def pack(c, e, sel32, send):
+    low = iota((KMAX, LANES), 1) < SUB
     for d in range(32):
-        even = sel32[pl.ds(2 * d, 16, stride=SUB), :]
-        odd = sel32[pl.ds(2 * d + 1, 16, stride=SUB), :]
-        put(d, 0, jnp.where(low, even, pltpu.roll(odd, SUB, 1)).astype(BF))
-        put(d, 1, jnp.where(low, pltpu.roll(even, SUB, 1), odd).astype(BF))
+        even = sel32[pl.ds(e * (KMAX * SUB) + 2 * d, KMAX, stride=SUB), :]
+        odd = sel32[pl.ds(e * (KMAX * SUB) + 2 * d + 1, KMAX, stride=SUB), :]
+        send[c, d, e, 0] = jnp.where(low, even, pltpu.roll(odd, SUB, 1)).astype(BF)
+        send[c, d, e, 1] = jnp.where(low, pltpu.roll(even, SUB, 1), odd).astype(BF)
 
 
 def iota(shape, dim):
@@ -99,7 +99,7 @@
         parts = []
         for p in range(2):
             for e2 in range(2):
-                parts.append(x32[pl.ds(p * 16 + 2 * j + e2, 32, stride=32), :].astype(BF))
+                parts.append(x32[pl.ds(e2 * 16 + p * KMAX + j, 32, stride=32), :].astype(BF))
         o32[pl.ds(j, LANES, stride=KMAX), :] = mm(kc, jnp.concatenate(parts, 0))
     put(o32[...].astype(BF))
 
@@ -133,36 +133,34 @@
         return carry
 
     lax.fori_loop(1, 32, greet, 0)
-    build_kernels(screened, kmat)
     pl.semaphore_wait(barrier, 33)
 
     halos = [
         pltpu.make_async_remote_copy(
-            s.at[:, :, pl.ds(source, 1)], sx.at[:, :, pl.ds(target, 1)], halo_send.at[k], halo_recv.at[k],
-            device_id=(me, where), device_id_type=MESH,
+            s.at[:, pl.ds(e, 1), pl.ds(source, 1)], sx.at[:, pl.ds(e, 1), pl.ds(target, 1)],
+            halo_send.at[e, k], halo_recv.at[e, k], device_id=(me, where), device_id_type=MESH,
         )
+        for e in range(2)
         for k, (source, target, where) in enumerate(((3, 0, up), (0, 5, down)))
     ]
     for halo in halos:
         halo.start()
     own.wait()
 
-    def send_cell(c):
-        def put(d, p, value):
-            send_a[c, d, p] = value
-
-        pack(sel32, put)
-        pltpu.make_async_copy(send_a.at[c, me], recv_a.at[c, me], a_recv.at[c]).start()
-
-        def push(k, carry):
+    def push(c, outgoing, arriving):
+        pltpu.make_async_copy(outgoing(me), arriving, a_recv.at[c]).start()
+
+        def one(k, carry):
             to = lax.rem(me + k, 32)
             pltpu.make_async_remote_copy(
-                send_a.at[c, to], recv_a.at[c, me], a_send.at[c], a_recv.at[c],
-                device_id=(to, z), device_id_type=MESH,
+                outgoing(to), arriving, a_send.at[c], a_recv.at[c], device_id=(to, z), device_id_type=MESH
             ).start()
             return carry
 
-        lax.fori_loop(1, 32, push, 0)
+        lax.fori_loop(1, 32, one, 0)
+
+    def send_cell(c):
+        push(c, lambda d: send_a.at[c, d], recv_a.at[c, me])
 
     def convolve(c):
         pltpu.make_async_copy(recv_a.at[c], recv_a.at[c], a_recv.at[c]).wait()
@@ -184,18 +182,25 @@
 
         lax.fori_loop(1, 32, push, 0)
 
+    def both(work):
+        def energy(e, carry):
+            work(e)
+            return carry
+
+        lax.fori_loop(0, 2, energy, 0)
+
     def inner_cell(i, carry):
         c = 1 + i
         for copy in inputs(c):
             copy.wait()
 
-        def energy(e, carry):
+        def work(e):
             total = side(c, e, 0, c + 1, vg, sx) + side(c, e, 1, c, vg, sx) + side(c, e, 2, c + 2, vg, sx)
             store_blocks(total, part.at[0, e])
             select(c, e, kept, count, part.at[0, e], sel32)
-            return carry
-
-        lax.fori_loop(0, 2, energy, 0)
+            pack(c, e, sel32, send_a)
+
+        both(work)
         send_cell(c)
         return carry
 
@@ -204,42 +209,63 @@
         for copy in inputs(c):
             copy.wait()
 
-        def energy(e, carry):
+        def work(e):
             store_blocks(side(c, e, 0, c + 1, vg, sx) + side(c, e, 2 - i, 2 + i, vg, sx), part.at[i, e])
+
+        both(work)
+
+        @pl.when(z == 7 * i)
+        def _():
+            def finish(e):
+                select(c, e, kept, count, part.at[i, e], sel32)
+                pack(c, e, sel32, send_a)
+
+            both(finish)
+            send_cell(c)
+
+        return carry
+
+    def edge_end(e):
+        def one(i, carry):
+            c = 3 * i
+
+            @pl.when(z != 7 * i)
+            def _():
+                total = side(c, e, 1 + i, 5 * i, vg, sx)
+                for rb in range(ORB // SUB):
+                    for cb in range(ORB // SUB):
+                        block = total[rb * SUB : (rb + 1) * SUB, cb * LANES : (cb + 1) * LANES]
+                        part[i, e, rb * 4 + cb] += block
+                select(c, e, kept, count, part.at[i, e], sel32)
+                pack(c, e, sel32, send_a)
+                push(c, lambda d: send_a.at[c, d, e], recv_a.at[c, me, e])
+
             return carry
 
-        lax.fori_loop(0, 2, energy, 0)
-        convolve(1 + i)
-        return carry
-
-    def edge_end(i, carry):
-        c = 3 * i
-        inside = jnp.where(z == 7 * i, 0.0, 1.0).astype(BF)
-
-        def energy(e, carry):
-            at = 5 * i
-            total = one_side(vg[1 + i, 0, e, c], vg[1 + i, 1, e, c], sx[0, e, at] * inside, sx[1, e, at] * inside)
-            for rb in range(ORB // SUB):
-                for cb in range(ORB // SUB):
-                    block = total[rb * SUB : (rb + 1) * SUB, cb * LANES : (cb + 1) * LANES]
-                    part[i, e, rb * 4 + cb] += block
-            select(c, e, kept, count, part.at[i, e], sel32)
-            return carry
-
-        lax.fori_loop(0, 2, energy, 0)
-        send_cell(c)
-        return carry
+        lax.fori_loop(0, 2, one, 0)
+
+    lax.fori_loop(0, 2, inner_cell, 0)
+    build_kernels(screened, kmat)
+    lax.fori_loop(0, 2, edge_start, 0)
+
+    def tail(e, carry):
+        for k in range(2):
+            pltpu.make_async_copy(
+                sx.at[:, pl.ds(e, 1), pl.ds(5 * k, 1)], sx.at[:, pl.ds(e, 1), pl.ds(5 * k, 1)], halo_recv.at[e, k]
+            ).wait()
+        edge_end(e)
+        convolve(1 + e)
+        return carry
+
+    lax.fori_loop(0, 2, tail, 0)
 
     def edge_convolve(i, carry):
         convolve(3 * i)
         return carry
 
-    lax.fori_loop(0, 2, inner_cell, 0)
-    lax.fori_loop(0, 2, edge_start, 0)
+    lax.fori_loop(0, 2, edge_convolve, 0)
     for halo in halos:
-        halo.wait()
-    lax.fori_loop(0, 2, edge_end, 0)
-    lax.fori_loop(0, 2, edge_convolve, 0)
+        halo.wait_send()
     for c in range(4):
         pltpu.make_async_copy(out.at[:, c], out.at[:, c], b_recv.at[c]).wait()
         sent = send_a.at[c, pl.ds(0, 31)]
@@ -266,16 +292,16 @@
             pltpu.VMEM((2, 2, 6, ORB, ORB), BF),
             pltpu.VMEM((2, 2, 16, SUB, LANES), F32),
             pltpu.VMEM((16 * SUB, LANES), F32),
-            pltpu.VMEM((4, 32, 2, 16, LANES), BF),
-            pltpu.VMEM((4, 32, 2, 16, LANES), BF),
+            pltpu.VMEM((4, 32, 2, 2, KMAX, LANES), BF),
+            pltpu.VMEM((4, 32, 2, 2, KMAX, LANES), BF),
             pltpu.VMEM((4, LANES, LANES), BF),
             pltpu.VMEM((32 * 32, LANES), F32),
             pltpu.VMEM((LANES * KMAX, LANES), F32),
             pltpu.VMEM((4, 32, 4, KMAX, LANES), BF),
             dma((4, 3)),
             dma(()),
-            dma((2,)),
-            dma((2,)),
+            dma((2, 2)),
+            dma((2, 2)),
             dma((4,)),
             dma((4,)),
             dma((4,)),

time: 45.3 us -> 41.6 us (0.918)
  Pallas kernels: 44.2 us -> 40 us
    pallas_call x1, Pallas kernels: 44.2 us -> 40 us  [per_device(): pl.pallas_call(whole, out_shape=pltpu.VMEM((4, 4, KMAX, SUB * SUB), BF),...]
where the time goes in v4:
time: 41.6 us; the launch traced here: 41 us
  Pallas kernels  40 us (96%)
  local copies, waits for them, and re-layouts  0.97 us (2%)
    pallas_call x1, Pallas kernels, per_device(): pl.pallas_call(whole, out_shape=pltpu.VMEM((4, 4, KMAX, SUB * SUB), BF),...  40 us
    unnamed x1, local copies, waits for them, and re-layouts  0.97 us

profile of v4, /device:TPU:1, one launch (start us, length us, event | category | flops | bytes accessed | tf_op | source)
XLA Modules:
  0.0 41.0 jit_solution(17594990391264128076)
XLA Ops:
  0.0 40.0 %whole.1 = bf16[4,4,8,4096]{3,2,1,0:T(8,128)(2,1)S(1)} custom-call(s32[4,8]{1,0:T(4,128)} %kept.1, s32[4]{0:T(128)} %count.1, bf16[2,4,128]{2,1,0:T(4,128)(2,1)} %screened.1, bf16[2,2,4,256,256]{4,3,2,1,0:T(8,128)(2,1)} %gd.1, bf16[2,2,4,256,256]{4,3,2,1,0:T(8,128)(2,1)} %gl.1, bf16[2,2,4,256,256]{4,3,2,1,0:T(8,128)(2,1)} %gu.1, bf16[2,2,4,256,256]{4,3,2,1,0:T(8,128)(2,1)} %s.1), custom_call_target="tpu_custom_call" | custom-call | tf_op jit(solution)/shard_map/whole/pallas_call | solution.py:285
  40.0 1.0 %copy.9 = bf16[2,2,4,8,4096]{4,3,2,1,0:T(8,128)(2,1)} copy(bf16[2,2,4,8,4096]{4,3,2,1,0:T(8,128)(2,1)S(1)} %bitcast.1) | data formatting | bytes 2097152

commit v5 on v4

--- a/solution.py
+++ b/solution.py
@@ -104,10 +104,19 @@
     put(o32[...].astype(BF))
 
 
+def far_first(me):
+    x, y, core = me // 8, me // 2 % 4, me % 2
+    hops = (0, 1, 2, 1)
+    steps = [(a, b, c) for a in range(4) for b in range(4) for c in range(2)][1:]
+    steps.sort(key=lambda o: (-hops[o[0]] - hops[o[1]], o))
+    return [(x + a) % 4 * 8 + (y + b) % 4 * 2 + (core + c) % 2 for a, b, c in steps]
+
+
 def whole(kept, count, screened, gd, gl, gu, s, out, vg, sx, part, sel32, send_a, recv_a, kmat, x32, o32, send_b,
           in_sem, s_sem, halo_send, halo_recv, a_send, a_recv, b_send, b_recv):
     me = lax.axis_index("energy")
     z = lax.axis_index("cell")
+    targets = far_first(me)
     up = lax.rem(z + 1, 8)
     down = lax.rem(z + 7, 8)
 
@@ -145,22 +154,19 @@
     ]
     for halo in halos:
         halo.start()
+    build_kernels(screened, kmat)
     own.wait()
 
-    def push(c, outgoing, arriving):
-        pltpu.make_async_copy(outgoing(me), arriving, a_recv.at[c]).start()
-
-        def one(k, carry):
-            to = lax.rem(me + k, 32)
+    def send_energy(c, e, source):
+        select(c, e, kept, count, source, sel32)
+        pack(c, e, sel32, send_a)
+        pltpu.make_async_copy(send_a.at[c, me, e], recv_a.at[c, me, e], a_recv.at[c]).start()
+
+        for to in targets:
             pltpu.make_async_remote_copy(
-                outgoing(to), arriving, a_send.at[c], a_recv.at[c], device_id=(to, z), device_id_type=MESH
+                send_a.at[c, to, e], recv_a.at[c, me, e], a_send.at[c], a_recv.at[c],
+                device_id=(to, z), device_id_type=MESH,
             ).start()
-            return carry
-
-        lax.fori_loop(1, 32, one, 0)
-
-    def send_cell(c):
-        push(c, lambda d: send_a.at[c, d], recv_a.at[c, me])
 
     def convolve(c):
         pltpu.make_async_copy(recv_a.at[c], recv_a.at[c], a_recv.at[c]).wait()
@@ -172,15 +178,11 @@
         mine = pl.ds(pl.multiple_of(me * LANES, LANES), LANES)
         pltpu.make_async_copy(send_b.at[c, me], out.at[:, c, :, mine], b_recv.at[c]).start()
 
-        def push(k, carry):
-            to = lax.rem(me + k, 32)
+        for to in targets:
             pltpu.make_async_remote_copy(
                 send_b.at[c, to], out.at[:, c, :, mine], b_send.at[c], b_recv.at[c],
                 device_id=(to, z), device_id_type=MESH,
             ).start()
-            return carry
-
-        lax.fori_loop(1, 32, push, 0)
 
     def both(work):
         def energy(e, carry):
@@ -197,11 +199,9 @@
         def work(e):
             total = side(c, e, 0, c + 1, vg, sx) + side(c, e, 1, c, vg, sx) + side(c, e, 2, c + 2, vg, sx)
             store_blocks(total, part.at[0, e])
-            select(c, e, kept, count, part.at[0, e], sel32)
-            pack(c, e, sel32, send_a)
+            send_energy(c, e, part.at[0, e])
 
         both(work)
-        send_cell(c)
         return carry
 
     def edge_start(i, carry):
@@ -216,12 +216,11 @@
 
         @pl.when(z == 7 * i)
         def _():
-            def finish(e):
-                select(c, e, kept, count, part.at[i, e], sel32)
-                pack(c, e, sel32, send_a)
-
-            both(finish)
-            send_cell(c)
+            both(lambda e: send_energy(c, e, part.at[i, e]))
+
+        @pl.when(i == 0)
+        def _():
+            convolve(1)
 
         return carry
 
@@ -236,16 +235,13 @@
                     for cb in range(ORB // SUB):
                         block = total[rb * SUB : (rb + 1) * SUB, cb * LANES : (cb + 1) * LANES]
                         part[i, e, rb * 4 + cb] += block
-                select(c, e, kept, count, part.at[i, e], sel32)
-                pack(c, e, sel32, send_a)
-                push(c, lambda d: send_a.at[c, d, e], recv_a.at[c, me, e])
+                send_energy(c, e, part.at[i, e])
 
             return carry
 
         lax.fori_loop(0, 2, one, 0)
 
     lax.fori_loop(0, 2, inner_cell, 0)
-    build_kernels(screened, kmat)
     lax.fori_loop(0, 2, edge_start, 0)
 
     def tail(e, carry):
@@ -254,16 +250,15 @@
                 sx.at[:, pl.ds(e, 1), pl.ds(5 * k, 1)], sx.at[:, pl.ds(e, 1), pl.ds(5 * k, 1)], halo_recv.at[e, k]
             ).wait()
         edge_end(e)
-        convolve(1 + e)
         return carry
 
     lax.fori_loop(0, 2, tail, 0)
 
-    def edge_convolve(i, carry):
-        convolve(3 * i)
-        return carry
-
-    lax.fori_loop(0, 2, edge_convolve, 0)
+    def last_cells(i, carry):
+        convolve(jnp.where(i == 0, 2, 3 * i - 3))
+        return carry
+
+    lax.fori_loop(0, 3, last_cells, 0)
     for halo in halos:
         halo.wait_send()
     for c in range(4):

time: 41.6 us -> 40.3 us (0.969); the launches traced: 41 us -> 40.2 us
  Pallas kernels: 40 us -> 39.2 us
    pallas_call x1, Pallas kernels: 40 us -> 39.2 us  [per_device(): pl.pallas_call(whole, out_shape=pltpu.VMEM((4, 4, KMAX, SUB * SUB), BF),...]
where the time goes in v5:
time: 40.3 us; the launch traced here: 40.2 us
  Pallas kernels  39.2 us (97%)
  local copies, waits for them, and re-layouts  0.97 us (2%)
    pallas_call x1, Pallas kernels, per_device(): pl.pallas_call(whole, out_shape=pltpu.VMEM((4, 4, KMAX, SUB * SUB), BF),...  39.2 us
    unnamed x1, local copies, waits for them, and re-layouts  0.97 us

profile of v5, /device:TPU:1, one launch (start us, length us, event | category | flops | bytes accessed | tf_op | source)
XLA Modules:
  0.0 40.2 jit_solution(6740284596866332216)
XLA Ops:
  0.0 39.2 %whole.1 = bf16[4,4,8,4096]{3,2,1,0:T(8,128)(2,1)S(1)} custom-call(s32[4,8]{1,0:T(4,128)} %kept.1, s32[4]{0:T(128)} %count.1, bf16[2,4,128]{2,1,0:T(4,128)(2,1)} %screened.1, bf16[2,2,4,256,256]{4,3,2,1,0:T(8,128)(2,1)} %gd.1, bf16[2,2,4,256,256]{4,3,2,1,0:T(8,128)(2,1)} %gl.1, bf16[2,2,4,256,256]{4,3,2,1,0:T(8,128)(2,1)} %gu.1, bf16[2,2,4,256,256]{4,3,2,1,0:T(8,128)(2,1)} %s.1), custom_call_target="tpu_custom_call" | custom-call | tf_op jit(solution)/shard_map/whole/pallas_call | solution.py:280
  39.2 1.0 %copy.9 = bf16[2,2,4,8,4096]{4,3,2,1,0:T(8,128)(2,1)} copy(bf16[2,2,4,8,4096]{4,3,2,1,0:T(8,128)(2,1)S(1)} %bitcast.1) | data formatting | bytes 2097152

commit v6 on v5

--- a/solution.py
+++ b/solution.py
@@ -142,6 +142,22 @@
         return carry
 
     lax.fori_loop(1, 32, greet, 0)
+
+    def three_sides(c, e):
+        total = side(c, e, 0, c + 1, vg, sx) + side(c, e, 1, c, vg, sx) + side(c, e, 2, c + 2, vg, sx)
+        store_blocks(total, part.at[0, e])
+
+    def first_cell(e, carry):
+        three_sides(1, e)
+        return carry
+
+    @pl.when(z == 0)
+    def _():
+        own.wait()
+        for copy in inputs(1):
+            copy.wait()
+        lax.fori_loop(0, 2, first_cell, 0)
+
     pl.semaphore_wait(barrier, 33)
 
     halos = [
@@ -155,7 +171,10 @@
     for halo in halos:
         halo.start()
     build_kernels(screened, kmat)
-    own.wait()
+
+    @pl.when(z != 0)
+    def _():
+        own.wait()
 
     def send_energy(c, e, source):
         select(c, e, kept, count, source, sel32)
@@ -193,12 +212,18 @@
 
     def inner_cell(i, carry):
         c = 1 + i
-        for copy in inputs(c):
-            copy.wait()
+        fresh = jnp.logical_or(z != 0, i == 1)
+
+        @pl.when(fresh)
+        def _():
+            for copy in inputs(c):
+                copy.wait()
 
         def work(e):
-            total = side(c, e, 0, c + 1, vg, sx) + side(c, e, 1, c, vg, sx) + side(c, e, 2, c + 2, vg, sx)
-            store_blocks(total, part.at[0, e])
+            @pl.when(fresh)
+            def _():
+                three_sides(c, e)
+
             send_energy(c, e, part.at[0, e])
 
         both(work)

time: 40.3 us -> 39.9 us (0.990)
  no operation moved by 1% of the time
where the time goes in v6:
time: 39.9 us; the launch traced here: 39.8 us
  Pallas kernels  38.8 us (97%)
  local copies, waits for them, and re-layouts  0.97 us (2%)
    pallas_call x1, Pallas kernels, per_device(): pl.pallas_call(whole, out_shape=pltpu.VMEM((4, 4, KMAX, SUB * SUB), BF),...  38.8 us
    unnamed x1, local copies, waits for them, and re-layouts  0.97 us

profile of v6, /device:TPU:1, one launch (start us, length us, event | category | flops | bytes accessed | tf_op | source)
XLA Modules:
  0.0 39.8 jit_solution(11489412955750886229)
XLA Ops:
  0.0 38.8 %whole.1 = bf16[4,4,8,4096]{3,2,1,0:T(8,128)(2,1)S(1)} custom-call(s32[4,8]{1,0:T(4,128)} %kept.1, s32[4]{0:T(128)} %count.1, bf16[2,4,128]{2,1,0:T(4,128)(2,1)} %screened.1, bf16[2,2,4,256,256]{4,3,2,1,0:T(8,128)(2,1)} %gd.1, bf16[2,2,4,256,256]{4,3,2,1,0:T(8,128)(2,1)} %gl.1, bf16[2,2,4,256,256]{4,3,2,1,0:T(8,128)(2,1)} %gu.1, bf16[2,2,4,256,256]{4,3,2,1,0:T(8,128)(2,1)} %s.1), custom_call_target="tpu_custom_call" | custom-call | tf_op jit(solution)/shard_map/whole/pallas_call | solution.py:305
  38.9 1.0 %copy.9 = bf16[2,2,4,8,4096]{4,3,2,1,0:T(8,128)(2,1)} copy(bf16[2,2,4,8,4096]{4,3,2,1,0:T(8,128)(2,1)S(1)} %bitcast.1) | data formatting | bytes 2097152
